TPU v7x, 128 devices: a whole 4x4x4 slice. The times are simulated.
128 devices in a mesh: rep: 2 (over x_hi), fsdp: 16 (over y, x_lo, core), tp: 4 (over z).
Axes of the slice: x: 4 (x_hi: 2, x_lo: 2; x = x_hi * 2 + x_lo), y: 4, z: 4, core: 2. Of those that a mesh axis runs over, the one named last changes fastest.
Arguments:
- gate_up_master: float32 [2, 4096, 14336], P(None, 'fsdp', ('rep', 'tp')), may hold values from -0.09375 to 0.09375
- gate_up_moment: float32 [2, 4096, 14336], P(None, 'fsdp', ('rep', 'tp')), may hold values from -0.00018310547 to 0.00018310547
- gate_up_second: float32 [2, 4096, 14336], P(None, 'fsdp', ('rep', 'tp')), may hold values from 8.5149493e-10 to 8.51495e-09
- gate_up_grad: bfloat16 [2, 4096, 14336], P(None, 'fsdp', ('rep', 'tp')), may hold values from -8 to 8
- down_master: float32 [4096, 14336], P('fsdp', ('rep', 'tp')), may hold values from -0.046875 to 0.046875
- down_moment: float32 [4096, 14336], P('fsdp', ('rep', 'tp')), may hold values from -0.00018310547 to 0.00018310547
- down_second: float32 [4096, 14336], P('fsdp', ('rep', 'tp')), may hold values from 8.5149493e-10 to 8.51495e-09
- down_grad: bfloat16 [4096, 14336], P('fsdp', ('rep', 'tp')), may hold values from -8 to 8
- norm_gain: float32 [4096], replicated, may hold values from 0.1 to 1.9
- start_rows: bfloat16 [1024, 4096], P(('rep', 'fsdp', 'tp')), may hold values from -6 to 6
- queries: bfloat16 [2, 1024, 4096], P(None, ('rep', 'fsdp', 'tp')), may hold values from -6 to 6
- new_kv: bfloat16 [2, 1024, 2, 1024], P(None, ('rep', 'fsdp', 'tp')), may hold values from -6 to 6
- kv_pool: bfloat16 [8192, 16, 2, 1024], P(('rep', 'fsdp', 'tp')), may hold values from -6 to 6
- page_table: int32 [1024, 8], P(('rep', 'fsdp', 'tp')), may hold values from 0 to 63, as said below
- cache_len: int32 [1024], P(('rep', 'fsdp', 'tp')), may hold values from 1 to 128, as said below
Outputs:
- final_rows: bfloat16 [1024, 4096], P(('rep', 'fsdp', 'tp'))
Inputs may be any that keep to these rules, and one draw needn't show every extreme that they name: `page_table`: within each aligned block of 8 rows, the entries name each of the 64 pages of that block exactly once. `cache_len`: some row has exactly 128 cached positions.
All inputs are finite; a program needn't handle non-finite values.
Results may differ from a plain program's by a relative error of at most 0.019.
Values may be sent and summed in bfloat16 or wider, within the bound.
No kernel may reach another device: no remote copies, remote signals or barrier semaphores. Data moves between devices by JAX's collectives and lax.ppermute only.
A program may use at most 128 MiB of HBM per device.

v0:
```python
import jax
import jax.numpy as jnp
from jax import lax
from jax.sharding import PartitionSpec as P

D = 4096
HD = 128
beta_one = 0.9
beta_two = 0.95
adam_eps = 1e-08
adam_time = 100.0
norm_eps = 1e-05


def adam_new(master, moment, second, grad, clip):
    learn_rate = 2.0 / D**0.5
    g = grad.astype(jnp.float32) * clip
    m = beta_one * moment + (1.0 - beta_one) * g
    v = beta_two * second + (1.0 - beta_two) * g * g
    first_fix = 1.0 - beta_one**adam_time
    second_fix = 1.0 - beta_two**adam_time
    return (master - learn_rate * (m / first_fix) / (jnp.sqrt(v / second_fix) + adam_eps)).astype(
        jnp.bfloat16
    )


def attend(query, keys, values, valid, fresh_k, fresh_v, step):
    scale = query.shape[-1] ** (-0.5)
    old = jnp.einsum("rjgh,rcjh->rjgc", query, keys, preferred_element_type=jnp.float32) * scale
    old = jnp.where(valid[:, None, None, :], old, -1e30)
    new = jnp.einsum("rjgh,srjh->rjgs", query, fresh_k, preferred_element_type=jnp.float32) * scale
    allowed = jnp.arange(fresh_k.shape[0]) <= step
    new = jnp.where(allowed[None, None, None, :], new, -1e30)
    top = jnp.maximum(jnp.max(old, axis=-1, keepdims=True), jnp.max(new, axis=-1, keepdims=True))
    exp_old = jnp.exp(old - top)
    exp_new = jnp.exp(new - top)
    total = jnp.sum(exp_old, axis=-1, keepdims=True) + jnp.sum(exp_new, axis=-1, keepdims=True)
    prob_old = (exp_old / total).astype(jnp.bfloat16)
    prob_new = (exp_new / total).astype(jnp.bfloat16)
    out = jnp.einsum("rjgc,rcjh->rjgh", prob_old, values, preferred_element_type=jnp.float32)
    out = out + jnp.einsum("rjgs,srjh->rjgh", prob_new, fresh_v, preferred_element_type=jnp.float32)
    return out.reshape(out.shape[0], -1)


def shards(
    gate_up_master,
    gate_up_moment,
    gate_up_second,
    gate_up_grad,
    down_master,
    down_moment,
    down_second,
    down_grad,
    norm_gain,
    start_rows,
    queries,
    new_kv,
    kv_pool,
    page_table,
    cache_len,
):
    local_squares = jnp.sum(jnp.square(gate_up_grad.astype(jnp.float32))) + jnp.sum(
        jnp.square(down_grad.astype(jnp.float32))
    )
    total = lax.psum(local_squares, ("rep", "fsdp", "tp"))
    clip = jnp.minimum(1.0, 1.0 / jnp.sqrt(total))
    gate_up = adam_new(gate_up_master, gate_up_moment, gate_up_second, gate_up_grad, clip)
    down_t = adam_new(down_master, down_moment, down_second, down_grad, clip)[None]
    n_fsdp = lax.axis_size("fsdp")
    n_rep = lax.axis_size("rep")
    cols = gate_up.shape[2]
    copied = (
        lax.all_gather(gate_up, "rep", axis=2, tiled=True),
        lax.all_gather(down_t, "rep", axis=2, tiled=True),
    )
    shaped = tuple(
        (a.reshape(a.shape[0], a.shape[1], n_rep, n_fsdp, cols // n_fsdp) for a in copied)
    )
    moved = (
        lax.all_to_all(shaped[0], "fsdp", split_axis=3, concat_axis=1, tiled=True),
        lax.all_to_all(shaped[1], "fsdp", split_axis=3, concat_axis=1, tiled=True),
    )
    weights = tuple((a.reshape(a.shape[0], a.shape[1], -1) for a in moved))
    roll_gate_up = weights[0]
    roll_down = weights[1][0]
    local_rows = start_rows.shape[0]
    kv_width = new_kv.shape[-1]
    head_dim = HD
    key_heads = kv_width // head_dim
    cache = kv_pool[page_table].reshape(local_rows, -1, 2, key_heads, head_dim)
    keys = cache[:, :, 0]
    values = cache[:, :, 1]
    valid = jnp.arange(keys.shape[1], dtype=jnp.int32)[None, :] < cache_len[:, None]
    fresh = new_kv.reshape(new_kv.shape[0], local_rows, 2, key_heads, head_dim)
    fresh_k = fresh[:, :, 0]
    fresh_v = fresh[:, :, 1]
    rows = start_rows
    for step in range(queries.shape[0]):
        query = queries[step].reshape(local_rows, key_heads, -1, head_dim)
        attended = attend(query, keys, values, valid, fresh_k, fresh_v, step)
        mixed = (rows.astype(jnp.float32) + attended).astype(jnp.bfloat16)
        mixed_f = mixed.astype(jnp.float32)
        normed = (
            mixed_f
            * lax.rsqrt(jnp.mean(mixed_f * mixed_f, axis=-1, keepdims=True) + norm_eps)
            * norm_gain
        ).astype(jnp.bfloat16)
        whole = lax.all_gather(normed, ("fsdp", "tp"), axis=0, tiled=True)
        gate = jnp.dot(whole, roll_gate_up[0], preferred_element_type=jnp.float32)
        upper = jnp.dot(whole, roll_gate_up[1], preferred_element_type=jnp.float32)
        hidden = (jax.nn.silu(gate) * upper).astype(jnp.bfloat16)
        summed = lax.psum_scatter(
            lax.dot_general(
                hidden, roll_down, (((1,), (1,)), ((), ())), preferred_element_type=jnp.float32
            ),
            ("fsdp", "tp"),
            scatter_dimension=0,
            tiled=True,
        )
        rows = (mixed_f + summed).astype(jnp.bfloat16)
    return rows


def solution(mesh):
    in_specs = (
        P(None, "fsdp", ("rep", "tp")),
        P(None, "fsdp", ("rep", "tp")),
        P(None, "fsdp", ("rep", "tp")),
        P(None, "fsdp", ("rep", "tp")),
        P("fsdp", ("rep", "tp")),
        P("fsdp", ("rep", "tp")),
        P("fsdp", ("rep", "tp")),
        P("fsdp", ("rep", "tp")),
        P(),
        P(("rep", "fsdp", "tp"), None),
        P(None, ("rep", "fsdp", "tp"), None),
        P(None, ("rep", "fsdp", "tp"), None, None),
        P(("rep", "fsdp", "tp"), None, None, None),
        P(("rep", "fsdp", "tp"), None),
        P(("rep", "fsdp", "tp")),
    )
    out_specs = P(("rep", "fsdp", "tp"), None)
    return jax.shard_map(shards, mesh=mesh, in_specs=in_specs, out_specs=out_specs, check_vma=False)
```

profile of v0, /device:TPU:0, one launch (start us, length us, event | category | flops | bytes accessed | tf_op | source)
XLA Modules:
  0.0 1184.5 jit_solution(11952147557319080114)
XLA Ops:
  6.5 1.5 copy.41
  8.0 1.2 fusion.20
  9.1 2.8 copy.40
  12.0 1.5 fusion.5
  14.8 68.2 %psum.7 = f32[]{:T(128)} all-reduce(f32[]{:T(128)S(6)} %add.102), channel_id=1, replica_groups=mesh['rep'=2,'fsdp'=16,'tp'=4] {'rep','fsdp','tp'}, use_global_device_ids=true, to_apply=%region_7.8 | all-reduce | flops 1 | bytes 8 | tf_op jit(solution)/shard_map/psum | solution.py:65
  83.7 2.8 copy.49
  86.5 2.8 copy.47
  89.2 2.7 copy.48
  91.9 5.0 fusion.25
  97.0 5.1 copy.43
  102.2 5.3 copy.39
  107.5 5.1 copy.42
  112.6 6.7 fusion.10
  119.8 12.9 %gather_fusion = bf16[64,16,2,1024]{3,2,1,0:T(2,128)(2,1)} fusion(bf16[64,16,2,1024]{3,2,1,0:T(2,128)(2,1)} %param.27, s32[1024]{0:T(1024)S(1)} %pad_clamp_fusion), kind=kCustom, calls=%fused_computation | custom fusion | bytes 8388864 | tf_op jit(solution)/shard_map/gather | solution.py:90
  132.7 7.8 reshape.110
  140.9 2.9 fusion.72
  143.9 1.3 fusion.78
  145.6 0.3 fusion.68
  145.9 0.7 fusion.30
  146.9 0.7 fusion.54
  147.6 2.9 copy.50
  150.6 3.7 all-to-all-start.1
  154.3 48.9 %all-gather.8.cloned.1.call-done = bf16[2,256,3584]{1,2,0:T(8,128)(2,1)} async-done(((bf16[2,256,1792]{1,2,0:T(8,128)(2,1)}), bf16[2,256,3584]{1,2,0:T(8,128)(2,1)}) %all-gather.8.cloned.1.call-update) | async-done | bytes 3670032 | tf_op jit(solution)/shard_map/all_gather | solution.py:73
  203.1 4.4 copy.44
  207.5 4.5 all-to-all-start
  212.3 1.0 copy.51
  213.4 0.8 copy.64
  214.2 45.9 %all-to-all-done = bf16[2,256,2,16,112]{1,4,2,0,3:T(8,128)(2,1)} async-done(((bf16[2,256,2,16,112]{1,4,2,0,3:T(8,128)(2,1)}), bf16[2,256,2,16,112]{1,4,2,0,3:T(8,128)(2,1)}, u32[]{:S(2)}, u32[]{:S(2)}) %all-to-all-start) | async-done | bytes 3670048 | tf_op jit(solution)/shard_map/all_to_all | solution.py:80
  260.1 2.3 fusion.73
  262.3 1.0 copy.45
  263.4 2.1 copy.62
  265.5 1.0 copy.46
  266.5 2.1 copy.63
  268.6 124.0 %all-gather.6.cloned.1.call-done = bf16[512,4096]{1,0:T(8,128)(2,1)} async-done(((bf16[8,4096]{1,0:T(8,128)(2,1)}), bf16[512,4096]{1,0:T(8,128)(2,1)}) %all-gather.6.cloned.1.call-update) | async-done | bytes 4194320 | tf_op jit(solution)/shard_map/all_gather | solution.py:108
  392.6 4.2 fusion.80
  396.9 8.7 fusion.27
  405.9 3.0 fusion.76
  409.3 0.3 fusion.69
  409.6 0.7 fusion.31
  410.4 294.7 %reduce-scatter.3.cloned.1.call-done = f32[8,4096]{1,0:T(8,128)} async-done(((f32[512,4096]{1,0:T(8,128)}), f32[8,4096]{1,0:T(8,128)}) %reduce-scatter.3.cloned.1.call-update) | async-done | bytes 131088 | tf_op jit(solution)/shard_map/reduce_scatter | solution.py:112
  705.2 1.1 fusion.56
  706.2 0.7 fusion.58
  707.0 0.3 reduce-scatter.5.cloned.1.call-start
  707.3 156.1 %all-gather.10.cloned.1.call-done = bf16[512,4096]{1,0:T(8,128)(2,1)} async-done(((bf16[8,4096]{1,0:T(8,128)(2,1)}), bf16[512,4096]{1,0:T(8,128)(2,1)}) %all-gather.10.cloned.1.call-update) | async-done | bytes 4194320 | tf_op jit(solution)/shard_map/all_gather | solution.py:108
  863.4 4.2 fusion.81
  867.6 8.8 fusion.29
  876.5 299.7 %reduce-scatter.5.cloned.1.call-done = f32[8,4096]{1,0:T(8,128)} async-done(((f32[512,4096]{1,0:T(8,128)}), f32[8,4096]{1,0:T(8,128)}) %reduce-scatter.5.cloned.1.call-update) | async-done | bytes 131088 | tf_op jit(solution)/shard_map/reduce_scatter | solution.py:112
  1176.1 1.5 fusion.59
  (57 shorter events, 2.7 us)
Async XLA Ops:
  6.5 141.1 %all-gather.12.cloned.1.call-start = ((), (), s32[]{:S(2)}) async-start(), calls=%async_computation.9 | async-start | bytes 2752512 | tf_op jit(solution)/shard_map/all_gather | solution.py:74
  97.0 106.2 %all-gather.8.cloned.1.call-start = ((), (), s32[]{:S(2)}) async-start(), calls=%async_computation.5 | async-start | bytes 5505024 | tf_op jit(solution)/shard_map/all_gather | solution.py:73
  112.6 7.0 copy-start.7
  112.6 7.1 copy-start.5
  112.6 7.1 copy-start.3
  119.3 273.3 %all-gather.6.cloned.1.call-start = ((), (), s32[]{:S(2)}) async-start(), calls=%async_computation.4 | async-start | bytes 4259840 | tf_op jit(solution)/shard_map/all_gather | solution.py:108
  132.7 7.8 copy-start.8
  143.9 2.0 copy-start.2
  143.9 2.0 copy-start
  145.9 0.8 copy-start.6
  145.9 1.0 copy-start.4
  150.6 56.9 %all-to-all-start.1 = ((bf16[1,256,2,16,112]{1,4,2,0,3:T(8,128)(2,1)}), bf16[1,256,2,16,112]{1,4,2,0,3:T(8,128)(2,1)S(1)}, u32[]{:S(2)}, u32[]{:S(2)}) async-start(bf16[1,256,2,16,112]{1,4,2,0,3:T(8,128)(2,1)} %copy.50), calls=%async_computation.1 | async-start | bytes 3670016 | tf_op jit(solution)/shard_map/all_to_all | solution.py:81
  207.5 52.5 %all-to-all-start = ((bf16[2,256,2,16,112]{1,4,2,0,3:T(8,128)(2,1)}), bf16[2,256,2,16,112]{1,4,2,0,3:T(8,128)(2,1)}, u32[]{:S(2)}, u32[]{:S(2)}) async-start(bf16[2,256,2,16,112]{1,4,2,0,3:T(8,128)(2,1)} %copy.44), calls=%async_computation | async-start | bytes 7340032 | tf_op jit(solution)/shard_map/all_to_all | solution.py:80
  212.1 493.1 %reduce-scatter.3.cloned.1.call-start = ((), (), s32[]{:S(2)}) async-start(), calls=%async_computation.6 | async-start | bytes 8519680 | tf_op jit(solution)/shard_map/reduce_scatter | solution.py:112
  405.5 457.9 %all-gather.10.cloned.1.call-start = ((), (), s32[]{:S(2)}) async-start(), calls=%async_computation.7 | async-start | bytes 4259840 | tf_op jit(solution)/shard_map/all_gather | solution.py:108
  405.9 3.7 copy-start.1
  707.0 469.2 %reduce-scatter.5.cloned.1.call-start = ((), (), s32[]{:S(2)}) async-start(), calls=%async_computation.8 | async-start | bytes 8519680 | tf_op jit(solution)/shard_map/reduce_scatter | solution.py:112
Sparse Core Ops, SparseCore 0:
  97.1 30.3 all-gather.11
  129.1 73.9 all-gather.7
  204.8 187.7 all-gather.5
  405.7 299.4 reduce-scatter.2
  707.1 156.2 all-gather.9
  876.6 299.5 reduce-scatter.4
where the time goes:
time: 1190 us; the launch traced here: 1180 us
  waiting for transfers between devices  969 us (81%)
  local copies, waits for them, and re-layouts  69.8 us (6%)
  blocking collectives  68.2 us (6%)
  matrix products  32.6 us (3%)
  other arithmetic  19.5 us (2%)
  between operations  15.8 us (1%)
    reduce_scatter x2, waiting for transfers between devices, shards(): lax.psum_scatter(lax.dot_general(hidden, roll_down, (((1,), (1,)), ((), (...  594 us
    all_gather x2, waiting for transfers between devices, shards(): whole = lax.all_gather(normed, ('fsdp', 'tp'), axis=0, tiled=True)  280 us
    psum x1, blocking collectives, shards(): total = lax.psum(local_squares, ('rep', 'fsdp', 'tp'))  68.2 us
    all_gather x1, waiting for transfers between devices, shards(): lax.all_gather(gate_up, 'rep', axis=2, tiled=True)  48.9 us
    all_to_all x1, waiting for transfers between devices, shards(): lax.all_to_all(shaped[0], 'fsdp', split_axis=3, concat_axis=1, tiled=True)  45.9 us
    unnamed x29, local copies, waits for them, and re-layouts  33.1 us
  transfers between devices with their start and end apart: 8, of which 6 were waited for; matrix products, arithmetic and copies ran while one was open for 6% of the time, Pallas kernels for 0%

commit v1 on v0

--- a/solution.py
+++ b/solution.py
@@ -70,7 +70,12 @@
     n_rep = lax.axis_size("rep")
     cols = gate_up.shape[2]
     copied = (
-        lax.all_gather(gate_up, "rep", axis=2, tiled=True),
+        jnp.concatenate(
+            lax.all_to_all(
+                jnp.stack([gate_up for _ in range(lax.axis_size("rep"))], axis=0), "rep", 0, 0
+            ),
+            axis=2,
+        ),
         lax.all_gather(down_t, "rep", axis=2, tiled=True),
     )
     shaped = tuple(

time: 1190 us -> 1130 us (0.950)
  waiting for transfers between devices: 969 us -> 904 us
    all_gather x2, waiting for transfers between devices: 280 us -> 193 us  [shards(): whole = lax.all_gather(normed, ('fsdp', 'tp'), axis=0, tiled=True)]
    all_gather x1 -> x0, waiting for transfers between devices: 48.9 us -> none  [shards(): lax.all_gather(gate_up, 'rep', axis=2, tiled=True)]
    all_to_all x0 -> x1, waiting for transfers between devices: none -> 46.3 us  [shards(): lax.all_to_all(jnp.stack([gate_up for _ in range(lax.axis_size('rep'))],...]
    all_to_all x1, waiting for transfers between devices: 0.01 us -> 23.2 us  [shards(): lax.all_to_all(shaped[1], 'fsdp', split_axis=3, concat_axis=1, tiled=True)]
  transfers between devices with their start and end apart: 8 -> 8, of which waited for: 6 -> 7; matrix products, arithmetic and copies ran while one was open for 6% -> 6% of each run, Pallas kernels for 0% -> 0%
where the time goes in v1:
time: 1130 us; the launch traced here: 1120 us
  waiting for transfers between devices  904 us (80%)
  local copies, waits for them, and re-layouts  68.9 us (6%)
  blocking collectives  68.2 us (6%)
  matrix products  32.5 us (3%)
  other arithmetic  20.8 us (2%)
  between operations  15.5 us (1%)
  starting transfers between devices  14.5 us (1%)
    reduce_scatter x2, waiting for transfers between devices, shards(): lax.psum_scatter(lax.dot_general(hidden, roll_down, (((1,), (1,)), ((), (...  596 us
    all_gather x2, waiting for transfers between devices, shards(): whole = lax.all_gather(normed, ('fsdp', 'tp'), axis=0, tiled=True)  193 us
    psum x1, blocking collectives, shards(): total = lax.psum(local_squares, ('rep', 'fsdp', 'tp'))  68.2 us
    all_to_all x1, waiting for transfers between devices, shards(): lax.all_to_all(jnp.stack([gate_up for _ in range(lax.axis_size('rep'))],...  46.3 us
    all_to_all x1, waiting for transfers between devices, shards(): lax.all_to_all(shaped[0], 'fsdp', split_axis=3, concat_axis=1, tiled=True)  45.4 us
    unnamed x29, local copies, waits for them, and re-layouts  32.9 us
    all_to_all x1, waiting for transfers between devices, shards(): lax.all_to_all(shaped[1], 'fsdp', split_axis=3, concat_axis=1, tiled=True)  23.2 us
  transfers between devices with their start and end apart: 8, of which 7 were waited for; matrix products, arithmetic and copies ran while one was open for 6% of the time, Pallas kernels for 0%

profile of v1, /device:TPU:0, one launch (start us, length us, event | category | flops | bytes accessed | tf_op | source)
XLA Modules:
  0.0 1124.4 jit_solution(13555531739420903412)
XLA Ops:
  6.5 1.5 copy.41
  8.0 1.2 fusion.20
  9.1 2.8 copy.40
  12.0 1.5 fusion.5
  14.8 68.2 %psum.7 = f32[]{:T(128)} all-reduce(f32[]{:T(128)S(6)} %add.102), channel_id=1, replica_groups=mesh['rep'=2,'fsdp'=16,'tp'=4] {'rep','fsdp','tp'}, use_global_device_ids=true, to_apply=%region_7.8 | all-reduce | flops 1 | bytes 8 | tf_op jit(solution)/shard_map/psum | solution.py:65
  83.7 2.8 copy.50
  86.5 2.7 copy.48
  89.2 2.7 copy.49
  92.0 5.1 fusion.25
  97.7 12.9 %gather_fusion = bf16[64,16,2,1024]{3,2,1,0:T(2,128)(2,1)} fusion(bf16[64,16,2,1024]{3,2,1,0:T(2,128)(2,1)} %param.27, s32[1024]{0:T(1024)S(1)} %pad_clamp_fusion), kind=kCustom, calls=%fused_computation | custom fusion | bytes 8388864 | tf_op jit(solution)/shard_map/gather | solution.py:95
  110.6 7.6 reshape.110
  118.2 2.5 fusion.73
  121.0 1.3 fusion.79
  123.0 0.7 fusion.31
  124.0 0.7 fusion.55
  124.7 5.1 copy.43
  129.8 5.1 copy.39
  135.0 5.1 copy.42
  140.1 5.7 fusion.26
  145.8 2.1 pad_maximum_fusion
  148.0 5.4 all-to-all-start
  153.4 2.9 copy.51
  156.3 46.3 %all-to-all-done = bf16[2,2,256,1792]{2,3,1,0:T(8,128)(2,1)} async-done(((bf16[2,2,256,1792]{2,3,1,0:T(8,128)(2,1)}), bf16[2,2,256,1792]{2,3,1,0:T(8,128)(2,1)}, u32[]{:S(2)}, u32[]{:S(2)}) %all-to-all-start) | async-done | bytes 3670048 | tf_op jit(solution)/shard_map/all_to_all | solution.py:74
  202.7 3.7 all-to-all-start.2
  206.4 4.3 copy.45
  210.7 23.2 %all-to-all-done.2 = bf16[1,256,2,16,112]{1,4,2,0,3:T(8,128)(2,1)S(1)} async-done(((bf16[1,256,2,16,112]{1,4,2,0,3:T(8,128)(2,1)}), bf16[1,256,2,16,112]{1,4,2,0,3:T(8,128)(2,1)S(1)}, u32[]{:S(2)}, u32[]{:S(2)}) %all-to-all-start.2) | async-done | bytes 1835040 | tf_op jit(solution)/shard_map/all_to_all | solution.py:86
  233.9 4.5 all-to-all-start.1
  238.7 1.0 copy.52
  239.7 0.8 copy.66
  240.6 45.4 %all-to-all-done.1 = bf16[2,256,2,16,112]{1,4,2,0,3:T(8,128)(2,1)} async-done(((bf16[2,256,2,16,112]{1,4,2,0,3:T(8,128)(2,1)}), bf16[2,256,2,16,112]{1,4,2,0,3:T(8,128)(2,1)}, u32[]{:S(2)}, u32[]{:S(2)}) %all-to-all-start.1) | async-done | bytes 3670048 | tf_op jit(solution)/shard_map/all_to_all | solution.py:85
  285.9 2.3 fusion.74
  288.2 1.0 copy.46
  289.3 2.0 copy.64
  291.3 1.0 copy.47
  292.3 2.1 copy.65
  294.4 37.3 %all-gather.5.cloned.1.call-done = bf16[512,4096]{1,0:T(8,128)(2,1)} async-done(((bf16[8,4096]{1,0:T(8,128)(2,1)}), bf16[512,4096]{1,0:T(8,128)(2,1)}) %all-gather.5.cloned.1.call-update) | async-done | bytes 4194320 | tf_op jit(solution)/shard_map/all_gather | solution.py:113
  331.7 4.2 fusion.81
  335.9 8.7 fusion.28
  345.0 3.0 fusion.77
  348.7 0.7 fusion.32
  349.5 296.4 %reduce-scatter.3.cloned.1.call-done = f32[8,4096]{1,0:T(8,128)} async-done(((f32[512,4096]{1,0:T(8,128)}), f32[8,4096]{1,0:T(8,128)}) %reduce-scatter.3.cloned.1.call-update) | async-done | bytes 131088 | tf_op jit(solution)/shard_map/reduce_scatter | solution.py:117
  645.9 1.1 fusion.57
  647.0 0.7 fusion.59
  648.0 155.7 %all-gather.7.cloned.1.call-done = bf16[512,4096]{1,0:T(8,128)(2,1)} async-done(((bf16[8,4096]{1,0:T(8,128)(2,1)}), bf16[512,4096]{1,0:T(8,128)(2,1)}) %all-gather.7.cloned.1.call-update) | async-done | bytes 4194320 | tf_op jit(solution)/shard_map/all_gather | solution.py:113
  803.7 4.2 fusion.82
  807.9 8.7 fusion.30
  816.6 299.7 %reduce-scatter.5.cloned.1.call-done = f32[8,4096]{1,0:T(8,128)} async-done(((f32[512,4096]{1,0:T(8,128)}), f32[8,4096]{1,0:T(8,128)}) %reduce-scatter.5.cloned.1.call-update) | async-done | bytes 131088 | tf_op jit(solution)/shard_map/reduce_scatter | solution.py:117
  1116.3 1.5 fusion.60
  (57 shorter events, 3.5 us)
Async XLA Ops:
  6.5 146.9 %all-gather.9.cloned.1.call-start = ((), (), s32[]{:S(2)}) async-start(), calls=%async_computation.9 | async-start | bytes 2752512 | tf_op jit(solution)/shard_map/all_gather | solution.py:79
  91.9 5.4 copy-start.8
  92.0 5.5 copy-start.7
  92.0 5.6 copy-start.5
  92.0 5.7 copy-start.3
  97.1 234.6 %all-gather.5.cloned.1.call-start = ((), (), s32[]{:S(2)}) async-start(), calls=%async_computation.5 | async-start | bytes 4259840 | tf_op jit(solution)/shard_map/all_gather | solution.py:113
  120.7 2.0 copy-start.2
  120.7 2.3 copy-start
  123.0 0.9 copy-start.6
  123.0 1.0 copy-start.4
  148.0 54.7 %all-to-all-start = ((bf16[2,2,256,1792]{2,3,1,0:T(8,128)(2,1)}), bf16[2,2,256,1792]{2,3,1,0:T(8,128)(2,1)}, u32[]{:S(2)}, u32[]{:S(2)}) async-start(bf16[2,2,256,1792]{2,3,1,0:T(8,128)(2,1)} %pad_maximum_fusion), calls=%async_computation | async-start | bytes 7340032 | tf_op jit(solution)/shard_map/all_to_all | solution.py:74
  202.7 31.3 %all-to-all-start.2 = ((bf16[1,256,2,16,112]{1,4,2,0,3:T(8,128)(2,1)}), bf16[1,256,2,16,112]{1,4,2,0,3:T(8,128)(2,1)S(1)}, u32[]{:S(2)}, u32[]{:S(2)}) async-start(bf16[1,256,2,16,112]{1,4,2,0,3:T(8,128)(2,1)} %copy.51), calls=%async_computation.2 | async-start | bytes 3670016 | tf_op jit(solution)/shard_map/all_to_all | solution.py:86
  233.9 52.0 %all-to-all-start.1 = ((bf16[2,256,2,16,112]{1,4,2,0,3:T(8,128)(2,1)}), bf16[2,256,2,16,112]{1,4,2,0,3:T(8,128)(2,1)}, u32[]{:S(2)}, u32[]{:S(2)}) async-start(bf16[2,256,2,16,112]{1,4,2,0,3:T(8,128)(2,1)} %copy.45), calls=%async_computation.1 | async-start | bytes 7340032 | tf_op jit(solution)/shard_map/all_to_all | solution.py:85
  238.4 407.4 %reduce-scatter.3.cloned.1.call-start = ((), (), s32[]{:S(2)}) async-start(), calls=%async_computation.6 | async-start | bytes 8519680 | tf_op jit(solution)/shard_map/reduce_scatter | solution.py:117
  344.6 459.1 %all-gather.7.cloned.1.call-start = ((), (), s32[]{:S(2)}) async-start(), calls=%async_computation.7 | async-start | bytes 4259840 | tf_op jit(solution)/shard_map/all_gather | solution.py:113
  345.0 3.7 copy-start.1
  647.7 468.6 %reduce-scatter.5.cloned.1.call-start = ((), (), s32[]{:S(2)}) async-start(), calls=%async_computation.8 | async-start | bytes 8519680 | tf_op jit(solution)/shard_map/reduce_scatter | solution.py:117
Sparse Core Ops, SparseCore 0:
  97.2 30.3 all-gather.8
  129.3 202.3 all-gather.4
  344.7 301.1 reduce-scatter.2
  647.8 155.8 all-gather.6
  816.8 299.5 reduce-scatter.4
